TPU v7x, 256 devices: a whole 4x4x8 slice. The times are simulated.
256 devices in a mesh: req: 4 (over x), blk: 64 (over z, y, core).
Axes of the slice: x: 4, y: 4, z: 8, core: 2. Of those that a mesh axis runs over, the one named last changes fastest.
Arguments:
- tokens: bfloat16 [4, 8192, 2048], P('req', 'blk'), may hold values from -6 to 6
- block_ids: int32 [4, 128], P('req', 'blk'), may hold values from 0 to 127, as said below
- lengths: int32 [4], P('req'), may hold values from 4097 to 8192, as said below
- page_table: int32 [4, 2, 128], P('req'), may hold values from 0 to 255, as said below
- qkv_weight: bfloat16 [2048, 3072], P(('req', 'blk')), may hold values from -0.125 to 0.125
- q_gain: float32 [256], replicated
- k_gain: float32 [256], replicated
Outputs:
- attended: bfloat16 [4, 8192, 2048], P('req', 'blk')
- kv_cache: bfloat16 [4, 256, 64, 512], P('req', 'blk')
Inputs may be any that keep to these rules, and one draw needn't show every extreme that they name: `lengths`: one prompt has length exactly 8192. `block_ids`: the two entries of one device are b and 127 - b; over a prompt the first entries are a permutation of 0 to 63. `page_table`: each prompt's entries are a permutation of 0 to 255.
All inputs are finite; a program needn't handle non-finite values.
Results may differ from a plain program's by a relative error of at most 0.013.
The roundings to bfloat16 on the way count: a program that leaves them out, or rounds other values in their place, can miss the bound.
Values may be sent and summed in bfloat16 or wider, within the bound.
A program may use at most 128 MiB of HBM per device.

v0:
```python
import math
import jax
import jax.numpy as jnp
from jax import lax
from jax.sharding import PartitionSpec as P

H = 8
KVH = 2
HD = 256
ROPE_BASE = 1000000.0
NORM_EPS = 1e-06
FLOOR_SCORE = -1e30


def head_norm(tensor, scale_gain):
    return (
        tensor
        * lax.rsqrt(jnp.mean(tensor * tensor, axis=-1, keepdims=True) + NORM_EPS)
        * scale_gain
    )


def rotary(tensor, positions):
    half_dim = tensor.shape[-1] // 2
    channel = jnp.arange(half_dim).astype(jnp.float32)
    inverse = jnp.power(jnp.float32(ROPE_BASE), -2.0 * channel / tensor.shape[-1])
    angles = positions.astype(jnp.float32)[:, None] * inverse[None, :]
    cosine = jnp.cos(angles)[:, None, :]
    sine_part = jnp.sin(angles)[:, None, :]
    front_half = tensor[..., :half_dim]
    second = tensor[..., half_dim:]
    return jnp.concatenate(
        [front_half * cosine - second * sine_part, second * cosine + front_half * sine_part], -1
    )


def body(tokens, block_ids, lengths, page_table, qkv_weight, q_gain, k_gain):
    local_rows = tokens[0]
    row_count = local_rows.shape[0]
    blk_rows = row_count // 2
    groups = H // KVH
    projected = jnp.dot(
        local_rows,
        lax.all_gather(qkv_weight, ("req", "blk"), axis=0, tiled=True),
        preferred_element_type=jnp.float32,
    )
    own_ids = block_ids[0]
    positions = (
        own_ids[:, None] * blk_rows + jnp.arange(blk_rows, dtype=jnp.int32)[None, :]
    ).reshape(row_count)
    length = lengths[0]
    query_raw = projected[:, : H * HD].reshape(row_count, H, HD)
    key_raw = projected[:, H * HD : (H + KVH) * HD].reshape(row_count, KVH, HD)
    value_raw = projected[:, (H + KVH) * HD :].reshape(row_count, KVH, HD)
    queries = (
        rotary(head_norm(query_raw, q_gain), positions)
        .astype(jnp.bfloat16)
        .reshape(row_count, KVH, groups, HD)
    )
    send_keys = (
        rotary(head_norm(key_raw, k_gain), positions)
        .astype(jnp.bfloat16)
        .reshape(row_count, KVH * HD)
    )
    send_values = head_norm(value_raw, 1.0).astype(jnp.bfloat16).reshape(row_count, KVH * HD)
    all_ids = lax.all_gather(block_ids, "blk", axis=1, tiled=True)[0]
    table_size = all_ids.shape[0]
    slot_count = page_table.shape[1] * page_table.shape[2] // lax.axis_size("blk")
    my_slots = lax.axis_index("blk") * slot_count + jnp.arange(slot_count, dtype=jnp.int32)
    slot_match = page_table[0][None, :, :] == my_slots[:, None, None]
    head_grid = jnp.arange(page_table.shape[1], dtype=jnp.int32)[None, :, None]
    block_grid = jnp.arange(page_table.shape[2], dtype=jnp.int32)[None, None, :]
    slot_head = jnp.sum(jnp.where(slot_match, head_grid, 0), axis=(1, 2))
    slot_block = jnp.sum(jnp.where(slot_match, block_grid, 0), axis=(1, 2))
    query_live = positions < length
    running_max = jnp.full((row_count, KVH, groups), FLOOR_SCORE, jnp.float32)
    running_sum = jnp.zeros((row_count, KVH, groups), jnp.float32)
    weighted = jnp.zeros((row_count, KVH, groups, HD), jnp.float32)
    pages_out = jnp.zeros((slot_count, blk_rows, 2 * HD), jnp.bfloat16)
    piece_keys = lax.all_gather(send_keys, "blk", axis=0, tiled=True)
    piece_values = lax.all_gather(send_values, "blk", axis=0, tiled=True)
    piece_rows = piece_keys.shape[0]
    global_rows = jnp.arange(piece_rows, dtype=jnp.int32)
    block_index = global_rows // blk_rows
    lookup = jnp.sum(
        jnp.where(
            block_index[:, None] == jnp.arange(table_size, dtype=jnp.int32)[None, :],
            all_ids[None, :],
            0,
        ),
        1,
    )
    key_pos = lookup * blk_rows + global_rows % blk_rows
    key_heads = piece_keys.reshape(piece_rows, KVH, HD)
    value_heads = piece_values.reshape(piece_rows, KVH, HD)
    key_block = math.gcd(piece_rows, 512)

    def one_block(block_number, running):
        block_keys = lax.dynamic_slice_in_dim(key_heads, block_number * key_block, key_block, 0)
        block_values = lax.dynamic_slice_in_dim(value_heads, block_number * key_block, key_block, 0)
        block_pos = lax.dynamic_slice_in_dim(key_pos, block_number * key_block, key_block, 0)
        allowed = (block_pos[None, :] <= positions[:, None]) & (block_pos[None, :] < length)
        old_max, old_sum, old_weighted = running
        scores = jnp.einsum(
            "rgad,kgd->rgak", queries, block_keys, preferred_element_type=jnp.float32
        )
        mask_full = allowed[:, None, None, :]
        new_max = jnp.maximum(old_max, jnp.max(jnp.where(mask_full, scores, FLOOR_SCORE), -1))
        rescale = jnp.exp(old_max - new_max)
        weights = jnp.where(mask_full, jnp.exp(scores - new_max[..., None]), 0.0)
        new_sum = old_sum * rescale + jnp.sum(weights, -1)
        product = jnp.einsum(
            "rgak,kgd->rgad",
            weights.astype(jnp.bfloat16),
            block_values,
            preferred_element_type=jnp.float32,
        )
        return (new_max, new_sum, old_weighted * rescale[..., None] + product)

    running_max, running_sum, weighted = lax.fori_loop(
        0, piece_rows // key_block, one_block, (running_max, running_sum, weighted)
    )
    paired = jnp.concatenate([key_heads, value_heads], -1)
    row_numbers = jnp.arange(piece_rows, dtype=jnp.int32)
    page_offsets = jnp.arange(blk_rows, dtype=jnp.int32)
    page_list = []
    for slot_number in range(slot_count):
        target = slot_block[slot_number] * blk_rows
        is_start = key_pos == target
        present = jnp.any(is_start)
        first_row = jnp.sum(jnp.where(is_start, row_numbers, 0))
        rows_here = lax.dynamic_slice_in_dim(paired, first_row, blk_rows, 0)
        chosen = lax.dynamic_index_in_dim(rows_here, slot_head[slot_number], 1, keepdims=False)
        live_rows = target + page_offsets < length
        chosen = jnp.where(live_rows[:, None], chosen, jnp.zeros_like(chosen))
        page_list.append(jnp.where(present, chosen, pages_out[slot_number]))
    running_max, running_sum, weighted, pages_out = (
        running_max,
        running_sum,
        weighted,
        jnp.stack(page_list),
    )
    divisor = jnp.where(query_live[:, None, None], running_sum, 1.0)
    attended = jnp.where(query_live[:, None, None, None], weighted / divisor[..., None], 0.0)
    attended = attended.reshape(row_count, H * HD).astype(jnp.bfloat16)
    return (attended[None], pages_out[None])


def solution(mesh):
    in_specs = (
        P("req", "blk", None),
        P("req", "blk"),
        P("req"),
        P("req", None, None),
        P(("req", "blk"), None),
        P(),
        P(),
    )
    out_specs = (P("req", "blk", None), P("req", "blk", None, None))
    return jax.shard_map(body, mesh=mesh, in_specs=in_specs, out_specs=out_specs, check_vma=False)
```

profile of v0, /device:TPU:1, one launch (start us, length us, event | category | flops | bytes accessed | tf_op | source)
XLA Modules:
  0.0 402.0 jit_solution(17340536434207153513)
XLA Ops:
  8.0 128.9 %all-gather.4.cloned.1.call-done = bf16[2048,3072]{1,0:T(8,128)(2,1)} async-done(((bf16[8,3072]{1,0:T(8,128)(2,1)}), bf16[2048,3072]{1,0:T(8,128)(2,1)}) %all-gather.4.cloned.1.call-update) | async-done | bytes 12582928 | tf_op jit(solution)/shard_map/all_gather | solution.py:44
  136.8 6.4 %fusion.21 = f32[128,3072]{1,0:T(8,128)S(1)} fusion(bf16[2048,3072]{1,0:T(8,128)(2,1)} %all-gather.4.cloned.1.call-done, bf16[1,128,2048]{2,1,0:T(8,128)(2,1)S(1)} %copy-done), kind=kOutput, calls=%fused_computation.43 | convolution fusion | flops 1610612736 | bytes 14680064 | tf_op jit(solution)/shard_map/dot_general | solution.py:42
  157.0 16.9 %all-reduce = s32[128]{0:T(128)S(1)} all-reduce(s32[128]{0:T(128)S(1)} %bitcast_dynamic-update-slice_fusion), channel_id=1, replica_groups=mesh['req'=4,'blk'=64] {'blk'}, use_global_device_ids=true, to_apply=%add | all-reduce | flops 128 | bytes 1024
  173.9 2.5 select_reduce_fusion
  192.6 32.3 %all-gather.8.cloned.1.call-done = bf16[8192,512]{1,0:T(8,128)(2,1)} async-done(((bf16[128,512]{1,0:T(8,128)(2,1)}), bf16[8192,512]{1,0:T(8,128)(2,1)}) %all-gather.8.cloned.1.call-update) | async-done | bytes 8388624 | tf_op jit(solution)/shard_map/all_gather | solution.py:81
  224.9 11.3 %copy.84 = bf16[8192,512]{0,1:T(8,128)(2,1)} copy(bf16[8192,512]{1,0:T(8,128)(2,1)} %all-gather.8.cloned.1.call-done) | data formatting | bytes 16777216
  236.2 74.7 %all-gather.6.cloned.1.call-done = bf16[8192,512]{0,1:T(8,128)(2,1)} async-done(((bf16[128,512]{0,1:T(8,128)(2,1)}), bf16[8192,512]{0,1:T(8,128)(2,1)}) %all-gather.6.cloned.1.call-update) | async-done | bytes 8388624 | tf_op jit(solution)/shard_map/all_gather | solution.py:80
  313.0 77.7 %while.18 = (s32[]{:T(128)}, f32[128,2,4]{0,2,1:T(4,128)S(1)}, f32[128,2,4]{0,2,1:T(4,128)S(1)}, f32[128,2,4,256]{0,3,2,1:T(8,128)S(1)}, s32[8192]{0:T(1024)S(1)...) while((s32[]{:T(128)}, f32[128,2,4]{0,2,1:T(4,128)S(1)}, ...), condition=%wide.region_7.8_spmd.clone, body=%wide.region_4.0_spmd.clone.sunk | while | flops 541988480 | bytes 10298591 | solution.py:120
  316.1 1.7 fusion.65
  321.0 1.7 fusion.65
  325.9 1.7 fusion.65
  330.7 1.7 fusion.65
  335.6 1.7 fusion.65
  340.4 1.7 fusion.65
  345.3 1.7 fusion.65
  350.2 1.7 fusion.65
  355.0 1.7 fusion.65
  359.9 1.7 fusion.65
  364.7 1.7 fusion.65
  369.6 1.7 fusion.65
  374.5 1.7 fusion.65
  379.3 1.7 fusion.65
  384.2 1.7 fusion.65
  389.0 1.7 fusion.65
  (227 shorter events, 67.6 us)
Async XLA Ops:
  7.2 129.7 %copy-start = (bf16[1,128,2048]{2,1,0:T(8,128)(2,1)S(1)}, bf16[1,128,2048]{2,1,0:T(8,128)(2,1)}, u32[]{:S(2)}) copy-start(bf16[1,128,2048]{2,1,0:T(8,128)(2,1)} %param.9) | copy-start | bytes 1572868
  7.2 129.6 %all-gather.4.cloned.1.call-start = ((), (), s32[]{:S(2)}) async-start(), calls=%async_computation | async-start | bytes 12632064 | tf_op jit(solution)/shard_map/all_gather | solution.py:44
  7.9 136.8 %copy-start.4 = (s32[1,2]{1,0:T(1,128)S(1)}, s32[1,2]{1,0:T(1,128)}, u32[]{:S(2)}) copy-start(s32[1,2]{1,0:T(1,128)} %param.10) | copy-start | bytes 28
  7.9 217.0 %all-gather.8.cloned.1.call-start = ((), (), s32[]{:S(2)}) async-start(), calls=%async_computation.2 | async-start | bytes 8519680 | tf_op jit(solution)/shard_map/all_gather | solution.py:81
  143.2 2.4 copy-start.1
  143.2 3.8 copy-start.3
  143.2 12.3 %copy-start.5 = (u32[256]{0:T(256)S(1)}, u32[256]{0:T(256)}, u32[]{:S(2)}) copy-start(u32[256]{0:T(256)} %constant.200) | copy-start | bytes 3076
  144.6 166.2 %all-gather.6.cloned.1.call-start = ((), (), s32[]{:S(2)}) async-start(), calls=%async_computation.1 | async-start | bytes 8519680 | tf_op jit(solution)/shard_map/all_gather | solution.py:80
  145.4 46.7 %copy-start.2 = (f32[256]{0:T(256)S(1)}, f32[256]{0:T(256)}, u32[]{:S(2)}) copy-start(f32[256]{0:T(256)} %param.14) | copy-start | bytes 3076
Sparse Core Ops, SparseCore 0:
  11.9 124.9 all-gather.3
  144.8 80.1 all-gather.7
  228.2 82.6 all-gather.5
where the time goes:
time: 404 us; the launch traced here: 402 us
  waiting for transfers between devices  237 us (59%)
  matrix products  59.4 us (15%)
  other arithmetic  37.3 us (9%)
  between operations  33 us (8%)
  local copies, waits for them, and re-layouts  17.7 us (4%)
  blocking collectives  16.9 us (4%)
    all_gather x1, waiting for transfers between devices, body(): lax.all_gather(qkv_weight, ('req', 'blk'), axis=0, tiled=True)  129 us
    all_gather x1, waiting for transfers between devices, body(): piece_keys = lax.all_gather(send_keys, 'blk', axis=0, tiled=True)  74.7 us
    all_gather x1, waiting for transfers between devices, body(): piece_values = lax.all_gather(send_values, 'blk', axis=0, tiled=True)  32.3 us
    dot_general x16, matrix products, one_block(): jnp.einsum('rgak,kgd->rgad', weights.astype(jnp.bfloat16), block_values,...  27.5 us
    dot_general x16, matrix products, one_block(): jnp.einsum('rgad,kgd->rgak', queries, block_keys, preferred_element_type=...  25.5 us
    unnamed x1, blocking collectives  16.9 us
    unnamed x18, local copies, waits for them, and re-layouts  12.4 us
    lt x16, other arithmetic, one_block(): block_pos[None, :] < length  11.6 us
  transfers between devices with their start and end apart: 3, of which 3 were waited for; matrix products, arithmetic and copies ran while one was open for 6% of the time, Pallas kernels for 0%

commit v1 on v0

--- a/solution.py
+++ b/solution.py
@@ -77,8 +77,13 @@
     running_sum = jnp.zeros((row_count, KVH, groups), jnp.float32)
     weighted = jnp.zeros((row_count, KVH, groups, HD), jnp.float32)
     pages_out = jnp.zeros((slot_count, blk_rows, 2 * HD), jnp.bfloat16)
-    piece_keys = lax.all_gather(send_keys, "blk", axis=0, tiled=True)
-    piece_values = lax.all_gather(send_values, "blk", axis=0, tiled=True)
+    piece_keys, piece_values = jnp.split(
+        jax.lax.all_gather(
+            jnp.concatenate([send_keys, send_values], axis=1), "blk", tiled=True, axis=0
+        ),
+        [send_keys.shape[1]],
+        axis=1,
+    )
     piece_rows = piece_keys.shape[0]
     global_rows = jnp.arange(piece_rows, dtype=jnp.int32)
     block_index = global_rows // blk_rows

time: 404 us -> 433 us (1.072)
  local copies, waits for them, and re-layouts: 17.7 us -> 85.4 us
  waiting for transfers between devices: 237 us -> 180 us
  matrix products: 59.4 us -> 75.6 us
    all_gather x2 -> x1, waiting for transfers between devices: 107 us -> 51.6 us  [body(): jax.lax.all_gather(jnp.concatenate([send_keys, send_values], axis=1), 'bl...]
    dynamic_slice x4 -> x32, local copies, waits for them, and re-layouts: 0.39 us -> 34.5 us  [one_block(): lax.dynamic_slice_in_dim(value_heads, block_number * key_block, key_block...]
    reshape x0 -> x2, local copies, waits for them, and re-layouts: none -> 19.7 us  [the longest x1 12.5 us: body(): value_heads = piece_values.reshape(piece_rows, KVH, HD)]
    dot_general x16, matrix products: 27.5 us -> 42.1 us  [one_block(): jnp.einsum('rgak,kgd->rgad', weights.astype(jnp.bfloat16), block_values,...]
    split x0 -> x1, local copies, waits for them, and re-layouts: none -> 11.4 us  [body(): jnp.split(jax.lax.all_gather(jnp.concatenate([send_keys, send_values], ax...]
    concatenate x1, local copies, waits for them, and re-layouts: 0.78 us -> 7.37 us  [body(): paired = jnp.concatenate([key_heads, value_heads], -1)]
    unnamed x18 -> x21, local copies, waits for them, and re-layouts: 12.4 us -> 8.42 us
  transfers between devices with their start and end apart: 3 -> 2, of which waited for: 3 -> 2; matrix products, arithmetic and copies ran while one was open for 6% -> 3% of each run, Pallas kernels for 0% -> 0%
where the time goes in v1:
time: 433 us; the launch traced here: 430 us
  waiting for transfers between devices  180 us (42%)
  local copies, waits for them, and re-layouts  85.4 us (20%)
  matrix products  75.6 us (17%)
  other arithmetic  39.2 us (9%)
  between operations  33 us (8%)
  blocking collectives  16.3 us (4%)
    all_gather x1, waiting for transfers between devices, body(): lax.all_gather(qkv_weight, ('req', 'blk'), axis=0, tiled=True)  128 us
    all_gather x1, waiting for transfers between devices, body(): jax.lax.all_gather(jnp.concatenate([send_keys, send_values], axis=1), 'bl...  51.6 us
    dot_general x16, matrix products, one_block(): jnp.einsum('rgak,kgd->rgad', weights.astype(jnp.bfloat16), block_values,...  42.1 us
    dynamic_slice x32, local copies, waits for them, and re-layouts, one_block(): lax.dynamic_slice_in_dim(value_heads, block_number * key_block, key_block...  34.5 us
    dot_general x16, matrix products, one_block(): jnp.einsum('rgad,kgd->rgak', queries, block_keys, preferred_element_type=...  27.1 us
    unnamed x1, blocking collectives  16.3 us
    reshape x1, local copies, waits for them, and re-layouts, body(): value_heads = piece_values.reshape(piece_rows, KVH, HD)  12.5 us
    lt x16, other arithmetic, one_block(): block_pos[None, :] < length  11.6 us
  transfers between devices with their start and end apart: 2, of which 2 were waited for; matrix products, arithmetic and copies ran while one was open for 3% of the time, Pallas kernels for 0%

profile of v1, /device:TPU:1, one launch (start us, length us, event | category | flops | bytes accessed | tf_op | source)
XLA Modules:
  0.0 430.3 jit_solution(9547353500871212083)
XLA Ops:
  9.2 127.7 %all-gather.3.cloned.1.call-done = bf16[2048,3072]{1,0:T(8,128)(2,1)} async-done(((bf16[8,3072]{1,0:T(8,128)(2,1)}), bf16[2048,3072]{1,0:T(8,128)(2,1)}) %all-gather.3.cloned.1.call-update) | async-done | bytes 12582928 | tf_op jit(solution)/shard_map/all_gather | solution.py:44
  136.8 6.4 %fusion.19 = f32[128,3072]{1,0:T(8,128)S(1)} fusion(bf16[2048,3072]{1,0:T(8,128)(2,1)} %all-gather.3.cloned.1.call-done, bf16[1,128,2048]{2,1,0:T(8,128)(2,1)S(1)} %copy-done), kind=kOutput, calls=%fused_computation.36 | convolution fusion | flops 1610612736 | bytes 14680064 | tf_op jit(solution)/shard_map/dot_general | solution.py:42
  148.6 16.3 %all-reduce = s32[128]{0:T(128)S(1)} all-reduce(s32[128]{0:T(128)S(1)} %bitcast_dynamic-update-slice_fusion.1), channel_id=1, replica_groups=mesh['req'=4,'blk'=64] {'blk'}, use_global_device_ids=true, to_apply=%add | all-reduce | flops 128 | bytes 1024
  191.2 51.6 %all-gather.5.cloned.1.call-done = bf16[8192,1024]{1,0:T(8,128)(2,1)} async-done(((bf16[128,1024]{1,0:T(8,128)(2,1)}), bf16[8192,1024]{1,0:T(8,128)(2,1)}) %all-gather.5.cloned.1.call-update) | async-done | bytes 16777232 | tf_op jit(solution)/shard_map/all_gather | solution.py:81
  242.8 11.4 %fusion.42 = (bf16[8192,512]{1,0:T(8,128)(2,1)}, bf16[8192,512]{1,0:T(8,128)(2,1)}) fusion(bf16[8192,1024]{1,0:T(8,128)(2,1)} %all-gather.5.cloned.1.call-done), kind=kLoop, calls=%fused_computation.103 | loop fusion | bytes 33554432 | tf_op jit(solution)/shard_map/split | solution.py:80
  254.2 7.1 %copy.72 = bf16[1024,2,8,256]{3,2,0,1:T(8,128)(2,1)} copy(bf16[1024,2,8,256]{3,2,1,0:T(8,128)(2,1)} %bitcast.107) | data formatting | bytes 16777216 | tf_op jit(solution)/shard_map/reshape | solution.py:99
  261.3 7.3 %constant_dynamic-update-slice_fusion = bf16[8192,2,512]{2,0,1:T(8,128)(2,1)} fusion(bf16[1024,2,8,256]{3,2,1,0:T(8,128)(2,1)} %bitcast.108), kind=kLoop, calls=%fused_computation.81 | loop fusion | bytes 16777216
  268.6 12.5 %reshape.385 = bf16[8192,2,256]{2,1,0:T(2,128)(2,1)} reshape(bf16[8192,512]{1,0:T(8,128)(2,1)} %get-tuple-element.301) | data formatting | bytes 16777216 | tf_op jit(solution)/shard_map/reshape | solution.py:100
  281.2 128.2 %while.18 = (s32[]{:T(128)}, f32[128,2,4]{0,2,1:T(4,128)S(1)}, f32[128,2,4]{0,2,1:T(4,128)S(1)}, f32[128,2,4,256]{0,3,2,1:T(8,128)}, s32[8192]{0:T(1024)S(1)}, /...) while((s32[]{:T(128)}, f32[128,2,4]{0,2,1:T(4,128)S(1)}, ...), condition=%wide.region_7.8_spmd.clone, body=%wide.region_4.0_spmd.clone.sunk | while | flops 541988480 | bytes 12395743 | solution.py:125
  293.4 2.7 fusion.61
  301.5 2.7 fusion.61
  309.6 2.7 fusion.61
  317.7 2.7 fusion.61
  325.8 2.7 fusion.61
  333.9 2.7 fusion.61
  341.9 2.7 fusion.61
  350.0 2.7 fusion.61
  358.1 2.7 fusion.61
  366.2 2.7 fusion.61
  374.3 2.7 fusion.61
  390.5 2.7 fusion.61
  406.7 2.7 fusion.61
  411.7 7.4 %bitcast_dynamic-update-slice_fusion = bf16[8192,2,512]{2,0,1:T(8,128)(2,1)} fusion(bf16[8192,2,512]{2,0,1:T(8,128)(2,1)} %constant_dynamic-update-slice_fusion, bf16[1024,2,8,256]{3,2,1,0:T(8,128)(2,1)} %bitcast.106), kind=kLoop, calls=%fused_computation.28 | loop fusion | bytes 16777216 | tf_op jit(solution)/shard_map/concatenate | solution.py:128
  419.1 3.6 fusion.24
  (255 shorter events, 110.0 us)
Async XLA Ops:
  7.2 129.7 %copy-start = (bf16[1,128,2048]{2,1,0:T(8,128)(2,1)S(1)}, bf16[1,128,2048]{2,1,0:T(8,128)(2,1)}, u32[]{:S(2)}) copy-start(bf16[1,128,2048]{2,1,0:T(8,128)(2,1)} %param.9) | copy-start | bytes 1572868
  7.2 129.6 %all-gather.3.cloned.1.call-start = ((), (), s32[]{:S(2)}) async-start(), calls=%async_computation | async-start | bytes 12632064 | tf_op jit(solution)/shard_map/all_gather | solution.py:44
  7.9 234.9 %all-gather.5.cloned.1.call-start = ((), (), s32[]{:S(2)}) async-start(), calls=%async_computation.1 | async-start | bytes 17039360 | tf_op jit(solution)/shard_map/all_gather | solution.py:81
  9.1 135.3 %copy-start.2 = (f32[256]{0:T(256)S(1)}, f32[256]{0:T(256)}, u32[]{:S(2)}) copy-start(f32[256]{0:T(256)} %param.15) | copy-start | bytes 3076
  9.1 136.6 %copy-start.4 = (s32[1,2,128]{2,1,0:T(2,128)S(1)}, s32[1,2,128]{2,1,0:T(2,128)}, u32[]{:S(2)}) copy-start(s32[1,2,128]{2,1,0:T(2,128)} %param.12) | copy-start | bytes 3076
  9.1 138.1 %copy-start.6 = (u32[256]{0:T(256)S(1)}, u32[256]{0:T(256)}, u32[]{:S(2)}) copy-start(u32[256]{0:T(256)} %constant.200) | copy-start | bytes 3076
  9.1 139.3 %copy-start.5 = (s32[1,2]{1,0:T(1,128)S(1)}, s32[1,2]{1,0:T(1,128)}, u32[]{:S(2)}) copy-start(s32[1,2]{1,0:T(1,128)} %param.10) | copy-start | bytes 28
  143.2 46.7 %copy-start.3 = (f32[256]{0:T(256)S(1)}, f32[256]{0:T(256)}, u32[]{:S(2)}) copy-start(f32[256]{0:T(256)} %param.14) | copy-start | bytes 3076
  411.7 11.7 %copy-start.1 = (bf16[1,128,2048]{2,1,0:T(8,128)(2,1)S(1)}, bf16[1,128,2048]{2,1,0:T(8,128)(2,1)}, u32[]{:S(2)}) copy-start(bf16[1,128,2048]{2,1,0:T(8,128)(2,1)} %param.9) | copy-start | bytes 1572868
Sparse Core Ops, SparseCore 0:
  11.9 124.9 all-gather.2
  145.8 97.0 all-gather.4
